TPU v7x, 32 devices: a whole 2x2x4 slice. The times are simulated.
32 devices in a mesh: space: 16 (over z, y, x), chan: 2 (over core).
Axes of the slice: x: 2, y: 2, z: 4, core: 2. Of those that a mesh axis runs over, the one named last changes fastest.
Arguments:
- source: bfloat16 [512, 48, 128], P('chan', 'space'), may hold values from -6 to 6
- kernel: bfloat16 [7, 7, 512, 512], P(None, None, 'chan'), may hold values from -0.0390625 to 0.0390625
Outputs:
- image: bfloat16 [512, 48, 128], P('chan', 'space')
All inputs are finite; a program needn't handle non-finite values.
Results may differ from a plain program's by a relative error of at most 0.001.
Values may be sent and summed in bfloat16 or wider, within the bound.
No kernel may reach another device: no remote copies, remote signals or barrier semaphores. Data moves between devices by JAX's collectives and lax.ppermute only.
A program may use at most 64 MiB of HBM per device.

v0:
```python
import jax
import jax.numpy as jnp
from jax import lax
from jax.sharding import PartitionSpec as P

OFF = 7


def padded_2(array, sides, width):
    for axis, dim in sides:
        devices, length = (lax.axis_size(axis), array.shape[dim])
        up = [(i, (i + 1) % devices) for i in range(devices - 1)]
        down = [(j, i) for i, j in up]
        last = lax.slice_in_dim(array, length - width, length, axis=dim)
        initial = lax.slice_in_dim(array, 0, width, axis=dim)
        before = lax.ppermute(last, axis, up)
        after = lax.ppermute(initial, axis, down)
        array = jnp.concatenate([before, array, after], axis=dim)
    return array


def correlate(kernel, padded, height):
    reach = (OFF - 1) // 2
    width_cols = padded.shape[2]
    widened = jnp.pad(padded, ((0, 0), (0, 0), (reach, reach)))
    total = jnp.zeros((kernel.shape[2], height, width_cols), jnp.float32)
    for row_shift in range(OFF):
        window = widened[:, row_shift : row_shift + height, :]
        stacked = jnp.stack(
            [window[:, :, col_shift : col_shift + width_cols] for col_shift in range(OFF)]
        )
        weights = kernel[row_shift]
        total = total + jnp.einsum(
            "boc,bcxy->oxy", weights, stacked, preferred_element_type=jnp.float32
        )
    return total


def shards(source, kernel):
    reach = (OFF - 1) // 2
    height = source.shape[1]
    gathered = lax.all_gather(source, "chan", axis=0, tiled=True)
    rimmed = padded_2(gathered, (("space", 1),), reach)
    coupled = correlate(kernel, rimmed, height)
    return (source.astype(jnp.float32) - coupled).astype(jnp.bfloat16)


def solution(mesh):
    placed = (P("chan", "space", None), P(None, None, "chan", None))
    return jax.shard_map(
        shards, mesh=mesh, in_specs=placed, out_specs=P("chan", "space", None), check_vma=False
    )
```

profile of v0, /device:TPU:0, one launch (start us, length us, event | category | flops | bytes accessed | tf_op | source)
XLA Modules:
  0.0 40.4 jit_solution(9014782237196229890)
XLA Ops:
  0.0 1.1 %copy.3 = bf16[256,3,128]{0,2,1:T(8,128)(2,1)S(1)} copy(bf16[256,3,128]{2,0,1:T(8,128)(2,1)} %param.2) | data formatting | bytes 393216 | tf_op args[0]
  1.1 2.2 %all_gather.3 = bf16[512,3,128]{0,2,1:T(8,128)(2,1)S(1)} all-gather(bf16[256,3,128]{0,2,1:T(8,128)(2,1)S(1)} %copy.3), channel_id=1, replica_groups=mesh['space'=16,'chan'=2] {'chan'}, dimensions={0}, use_global_device_ids=true | all-gather | bytes 589824 | tf_op jit(solution)/shard_map/all_gather | solution.py:42
  3.3 4.8 %collective-permute-start = (bf16[512,3,128]{0,2,1:T(8,128)(2,1)S(1)}, bf16[512,3,128]{0,2,1:T(8,128)(2,1)S(1)}, u32[]{:S(2)}, u32[]{:S(2)}) collective-permute-start(bf16[512,3,128]{0,2,1:T(8,128)(2,1)S(1)} %all_gather.3), channel_id=1, source_target_pairs={{0,2},{2,4},{4,6},{6,8},{8,10},{10,12},{12,14},{14,16},{16,18},{18... | collective-permute-start | bytes 1179656 | tf_op jit(solution)/shard_map/ppermute | solution.py:16
  8.0 1.3 %collective-permute-start.1 = (bf16[512,3,128]{0,2,1:T(8,128)(2,1)S(1)}, bf16[512,3,128]{0,2,1:T(8,128)(2,1)S(1)}, u32[]{:S(2)}, u32[]{:S(2)}) collective-permute-start(bf16[512,3,128]{0,2,1:T(8,128)(2,1)S(1)} %all_gather.3), channel_id=1, source_target_pairs={{2,0},{4,2},{6,4},{8,6},{10,8},{12,10},{14,12},{16,14},{18,16},{20... | collective-permute-start | bytes 1179656 | tf_op jit(solution)/shard_map/ppermute | solution.py:17
  9.3 15.8 %collective-permute-done = bf16[512,3,128]{0,2,1:T(8,128)(2,1)S(1)} collective-permute-done((bf16[512,3,128]{0,2,1:T(8,128)(2,1)S(1)}, bf16[512,3,128]{0,2,1:T(8,128)(2,1)S(1)}, u32[]{:S(2)}, u32[]{:S(2)}) %collective-permute-start) | collective-permute-done | bytes 393248 | tf_op jit(solution)/shard_map/ppermute | solution.py:16
  25.1 1.9 %collective-permute-done.1 = bf16[512,3,128]{0,2,1:T(8,128)(2,1)S(1)} collective-permute-done((bf16[512,3,128]{0,2,1:T(8,128)(2,1)S(1)}, bf16[512,3,128]{0,2,1:T(8,128)(2,1)S(1)}, u32[]{:S(2)}, u32[]{:S(2)}) %collective-permute-start.1) | collective-permute-done | bytes 393248 | tf_op jit(solution)/shard_map/ppermute | solution.py:17
  27.1 0.3 fusion.26
  27.4 0.2 fusion.80
  27.7 0.1 constant_dynamic-update-slice_fusion.3
  27.8 0.1 fusion.119
  27.9 0.1 fusion.118
  28.0 0.1 fusion.117
  28.1 0.1 fusion.116
  28.2 0.1 fusion.115
  28.3 0.0 slice-start
  28.3 0.4 fusion.79
  28.7 0.0 slice-start.1
  28.7 0.4 fusion.78
  29.1 0.2 fusion.84
  29.3 0.0 slice-start.2
  29.3 0.1 bitcast_dynamic-update-slice_fusion.1
  29.4 0.4 fusion.77
  29.7 0.0 slice-start.3
  29.7 0.4 fusion.76
  30.1 0.4 fusion.75
  30.5 0.0 slice-done
  30.5 1.4 %slice-done.1 = s8[4194304]{0:T(1024)(128)(4,1)S(1)} async-done(((s8[12845056]{0:T(1024)(128)(4,1)}), s8[4194304]{0:T(1024)(128)(4,1)S(1)}, s32[]{:S(2)}) %slice-start.1) | async-done | bytes 4194328
  31.9 1.3 %slice-done.2 = s8[4194304]{0:T(1024)(128)(4,1)S(1)} async-done(((s8[12845056]{0:T(1024)(128)(4,1)}), s8[4194304]{0:T(1024)(128)(4,1)S(1)}, s32[]{:S(2)}) %slice-start.2) | async-done | bytes 4194328
  33.2 0.0 slice-done.3
  33.2 0.9 %fusion.30 = f32[3,128,256]{2,1,0:T(8,128)S(1)} fusion(bf16[7,512,3,128]{1,3,2,0:T(8,128)(2,1)S(1)} %get-tuple-element.10, bf16[7,7,256,512]{3,2,1,0:T(8,128)(2,1)S(1)} %bitcast.321), kind=kOutput, calls=%fused_computation.30 | convolution fusion | flops 704643072 | bytes 4980736 | tf_op jit(solution)/shard_map/boc,bcxy->oxy/dot_general | solution.py:33
  34.1 0.9 %fusion.69 = f32[3,128,256]{2,1,0:T(8,128)S(1)} fusion(f32[3,128,256]{2,1,0:T(8,128)S(1)} %fusion.30, bf16[7,512,3,128]{1,3,0,2:T(8,128)(2,1)S(1)} %fusion.115, bf16[7,7,256,512]{3,2,1,0:T(8,128)(2,1)S(1)} %bitcast.321), kind=kOutput, calls=%fused_computation.43 | convolution fusion | flops 704741376 | bytes 5373952 | tf_op jit(solution)/shard_map/boc,bcxy->oxy/dot_general | solution.py:33
  35.0 0.9 %fusion.66 = f32[3,128,256]{2,1,0:T(8,128)S(1)} fusion(f32[3,128,256]{2,1,0:T(8,128)S(1)} %fusion.69, bf16[7,512,3,128]{1,3,2,0:T(8,128)(2,1)S(1)} %get-tuple-element.9, bf16[7,7,256,512]{3,2,1,0:T(8,128)(2,1)S(1)} %bitcast.321), kind=kOutput, calls=%fused_computation.42 | convolution fusion | flops 704741376 | bytes 5373952 | tf_op jit(solution)/shard_map/boc,bcxy->oxy/dot_general | solution.py:33
  35.9 0.9 %fusion.63 = f32[3,128,256]{2,1,0:T(8,128)S(1)} fusion(f32[3,128,256]{2,1,0:T(8,128)S(1)} %fusion.66, bf16[7,512,3,128]{1,3,2,0:T(8,128)(2,1)S(1)} %get-tuple-element.8, bf16[7,7,256,512]{3,2,1,0:T(8,128)(2,1)S(1)} %bitcast.321), kind=kOutput, calls=%fused_computation.41 | convolution fusion | flops 704741376 | bytes 5373952 | tf_op jit(solution)/shard_map/boc,bcxy->oxy/dot_general | solution.py:33
  36.9 0.9 %fusion.60 = f32[3,128,256]{2,1,0:T(8,128)S(1)} fusion(f32[3,128,256]{2,1,0:T(8,128)S(1)} %fusion.63, bf16[7,512,3,128]{1,3,2,0:T(8,128)(2,1)S(1)} %get-tuple-element.7, bf16[7,7,256,512]{3,2,1,0:T(8,128)(2,1)S(1)} %bitcast.321), kind=kOutput, calls=%fused_computation.40 | convolution fusion | flops 704741376 | bytes 5373952 | tf_op jit(solution)/shard_map/boc,bcxy->oxy/dot_general | solution.py:33
  37.8 0.9 %fusion.57 = f32[3,128,256]{2,1,0:T(8,128)S(1)} fusion(f32[3,128,256]{2,1,0:T(8,128)S(1)} %fusion.60, bf16[7,512,3,128]{1,3,2,0:T(8,128)(2,1)S(1)} %get-tuple-element.6, bf16[7,7,256,512]{3,2,1,0:T(8,128)(2,1)S(1)} %bitcast.321), kind=kOutput, calls=%fused_computation.39 | convolution fusion | flops 704741376 | bytes 5373952 | tf_op jit(solution)/shard_map/boc,bcxy->oxy/dot_general | solution.py:33
  38.7 0.9 %fusion.72 = bf16[256,3,128]{0,2,1:T(8,128)(2,1)S(1)} fusion(f32[3,128,256]{2,1,0:T(8,128)S(1)} %fusion.57, bf16[7,512,3,128]{1,3,2,0:T(8,128)(2,1)S(1)} %get-tuple-element.5, bf16[7,7,256,512]{3,2,1,0:T(8,128)(2,1)S(1)} %bitcast.321, bf16[256,3,128]{0,2,1:T(8,128)(2,1)S(1)} %copy.3), kind=kOutput, calls=%fused_computation.44 | convolution fusion | flops 705036288 | bytes 5373952 | tf_op jit(solution)/shard_map/boc,bcxy->oxy/dot_general | solution.py:33
  39.6 0.8 %copy.17 = bf16[256,3,128]{2,0,1:T(8,128)(2,1)} copy(bf16[256,3,128]{0,2,1:T(8,128)(2,1)S(1)} %fusion.72) | data formatting | bytes 393216 | tf_op jit(solution)/shard_map/convert_element_type | solution.py:45
  (5 shorter events, 0.1 us)
Async XLA Ops:
  3.3 21.8 %collective-permute-start = (bf16[512,3,128]{0,2,1:T(8,128)(2,1)S(1)}, bf16[512,3,128]{0,2,1:T(8,128)(2,1)S(1)}, u32[]{:S(2)}, u32[]{:S(2)}) collective-permute-start(bf16[512,3,128]{0,2,1:T(8,128)(2,1)S(1)} %all_gather.3), channel_id=1, source_target_pairs={{0,2},{2,4},{4,6},{6,8},{8,10},{10,12},{12,14},{14,16},{16,18},{18... | collective-permute-start | bytes 1179656 | tf_op jit(solution)/shard_map/ppermute | solution.py:16
  8.0 19.0 %collective-permute-start.1 = (bf16[512,3,128]{0,2,1:T(8,128)(2,1)S(1)}, bf16[512,3,128]{0,2,1:T(8,128)(2,1)S(1)}, u32[]{:S(2)}, u32[]{:S(2)}) collective-permute-start(bf16[512,3,128]{0,2,1:T(8,128)(2,1)S(1)} %all_gather.3), channel_id=1, source_target_pairs={{2,0},{4,2},{6,4},{8,6},{10,8},{12,10},{14,12},{16,14},{18,16},{20... | collective-permute-start | bytes 1179656 | tf_op jit(solution)/shard_map/ppermute | solution.py:17
  28.3 2.2 %slice-start = ((s8[12845056]{0:T(1024)(128)(4,1)}), s8[4194304]{0:T(1024)(128)(4,1)S(1)}, s32[]{:S(2)}) async-start(s8[12845056]{0:T(1024)(128)(4,1)} %bitcast.320), calls=%async_computation | async-start | bytes 8388608
  28.7 3.2 %slice-start.1 = ((s8[12845056]{0:T(1024)(128)(4,1)}), s8[4194304]{0:T(1024)(128)(4,1)S(1)}, s32[]{:S(2)}) async-start(s8[12845056]{0:T(1024)(128)(4,1)} %bitcast.320), calls=%async_computation.1 | async-start | bytes 8388608
  29.3 3.9 %slice-start.2 = ((s8[12845056]{0:T(1024)(128)(4,1)}), s8[4194304]{0:T(1024)(128)(4,1)S(1)}, s32[]{:S(2)}) async-start(s8[12845056]{0:T(1024)(128)(4,1)} %bitcast.320), calls=%async_computation.2 | async-start | bytes 8388608
  29.7 3.5 %slice-start.3 = ((s8[12845056]{0:T(1024)(128)(4,1)}), s8[262144]{0:T(1024)(128)(4,1)S(1)}, s32[]{:S(2)}) async-start(s8[12845056]{0:T(1024)(128)(4,1)} %bitcast.320), calls=%async_computation.3 | async-start | bytes 524288
where the time goes:
time: 40.6 us; the launch traced here: 40.4 us
  waiting for transfers between devices  17.7 us (44%)
  local copies, waits for them, and re-layouts  7.54 us (19%)
  matrix products  6.37 us (16%)
  starting transfers between devices  6.06 us (15%)
  blocking collectives  2.21 us (5%)
    ppermute x1, waiting for transfers between devices, padded_2(): before = lax.ppermute(last, axis, up)  15.8 us
    dot_general x7, matrix products, correlate(): jnp.einsum('boc,bcxy->oxy', weights, stacked, preferred_element_type=jnp....  6.37 us
    unnamed x24, local copies, waits for them, and re-layouts  6.25 us
    ppermute x1, starting transfers between devices, padded_2(): before = lax.ppermute(last, axis, up)  4.76 us
    all_gather x1, blocking collectives, shards(): gathered = lax.all_gather(source, 'chan', axis=0, tiled=True)  2.21 us
    ppermute x1, waiting for transfers between devices, padded_2(): after = lax.ppermute(initial, axis, down)  1.95 us
    ppermute x1, starting transfers between devices, padded_2(): after = lax.ppermute(initial, axis, down)  1.29 us
    convert_element_type x1, local copies, waits for them, and re-layouts, shards(): return (source.astype(jnp.float32) - coupled).astype(jnp.bfloat16)  0.82 us
  transfers between devices with their start and end apart: 2, of which 2 were waited for; matrix products, arithmetic and copies ran while one was open for 0% of the time, Pallas kernels for 0%

commit v1 on v0

--- a/solution.py
+++ b/solution.py
@@ -1,9 +1,18 @@
+import functools
+
 import jax
 import jax.numpy as jnp
 from jax import lax
+from jax.experimental import pallas as pl
+from jax.experimental.pallas import tpu as pltpu
 from jax.sharding import PartitionSpec as P
 
 OFF = 7
+REACH = (OFF - 1) // 2
+MXU = 256
+LANES = 128
+EDGE = 8
+UNITS = 2
 
 
 def padded_2(array, sides, width):
@@ -20,9 +29,8 @@
 
 
 def correlate(kernel, padded, height):
-    reach = (OFF - 1) // 2
     width_cols = padded.shape[2]
-    widened = jnp.pad(padded, ((0, 0), (0, 0), (reach, reach)))
+    widened = jnp.pad(padded, ((0, 0), (0, 0), (REACH, REACH)))
     total = jnp.zeros((kernel.shape[2], height, width_cols), jnp.float32)
     for row_shift in range(OFF):
         window = widened[:, row_shift : row_shift + height, :]
@@ -36,13 +44,201 @@
     return total
 
 
-def shards(source, kernel):
-    reach = (OFF - 1) // 2
+def general(source, kernel):
     height = source.shape[1]
     gathered = lax.all_gather(source, "chan", axis=0, tiled=True)
-    rimmed = padded_2(gathered, (("space", 1),), reach)
+    rimmed = padded_2(gathered, (("space", 1),), REACH)
     coupled = correlate(kernel, rimmed, height)
     return (source.astype(jnp.float32) - coupled).astype(jnp.bfloat16)
+
+
+def spread(block, row_of, pad, shifted):
+    rows = block.shape[0]
+    for q in range(rows):
+        turned = block[row_of(q)].astype(jnp.float32).T
+        for part in range(MXU // LANES):
+            lanes = slice(part * LANES, (part + 1) * LANES)
+            pad[q, part, pl.ds(EDGE, LANES), :] = turned[:, lanes]
+            for b in range(OFF):
+                view = pad[q, part, pl.ds(EDGE + b - REACH, LANES), :]
+                shifted[b, q, :, lanes] = view.astype(jnp.bfloat16)
+
+
+def clear_edges(pad):
+    rows, parts = pad.shape[:2]
+    blank = jnp.zeros((EDGE, LANES), jnp.float32)
+    for q in range(rows):
+        for part in range(parts):
+            pad[q, part, pl.ds(0, EDGE), :] = blank
+            pad[q, part, pl.ds(EDGE + LANES, EDGE), :] = blank
+
+
+def multiply(tiles, weights, shifted, sums):
+    rows = len(sums) // UNITS
+    load, stage = [0] * UNITS, [0] * UNITS
+    for n, a, half, b, pairs in tiles:
+        unit = load.index(min(load))
+        load[unit] += max(len(pairs), 2)
+        slot = stage[unit]
+        stage[unit] ^= 1
+        lanes = pl.ds(pl.multiple_of(half * MXU, MXU), MXU)
+        pltpu.matmul_push_rhs(
+            weights[a, b, :, lanes], staging_register=slot, mxu_index=unit, transpose=True
+        )
+        for order, (q, i) in enumerate(pairs):
+            pltpu.matmul_acc_lhs(
+                sums[unit * rows + i],
+                shifted[n, b, q],
+                load_staged_rhs=slot if order == 0 else None,
+            )
+
+
+def collect(sums, i):
+    rows = len(sums) // UNITS
+    value = pltpu.matmul_pop(sums[i])
+    for unit in range(1, UNITS):
+        value = value + pltpu.matmul_pop(sums[unit * rows + i])
+    return value
+
+
+def with_sums(rows, body):
+    refs = [
+        pltpu.ACC(unit)((LANES, MXU), jnp.float32) for unit in range(UNITS) for _ in range(rows)
+    ]
+    pl.run_scoped(lambda *sums: body(sums), *refs)
+
+
+def own_kernel(place, *refs):
+    *blocks, weights, total, pad, shifted = refs
+    rows = blocks[0].shape[0]
+
+    def body(sums):
+        clear_edges(pad)
+        tiles = []
+        for n, block in enumerate(blocks):
+            spread(block, lambda q: q, pad, shifted.at[n])
+            half = place[n]
+            for b in range(OFF):
+                for a in range(OFF):
+                    pairs = [(q, q - a + REACH) for q in range(rows)]
+                    pairs = [(q, i) for q, i in pairs if 0 <= i < rows]
+                    if pairs:
+                        tiles.append((n, a, half, b, pairs))
+        multiply(tiles, weights, shifted, sums)
+        for i in range(rows):
+            total[i] = collect(sums, i)
+
+    with_sums(rows, body)
+
+
+def halo_terms(place, blocks, halves, weights, pad, shifted, sums):
+    rows = blocks[0].shape[0]
+    flip = place[2]
+    clear_edges(pad)
+    tiles = []
+    for n, block in enumerate(blocks):
+        spread(block, lambda q: q + flip * (rows - 1 - 2 * q), pad, shifted.at[n])
+        for b in range(OFF):
+            for t in range(rows):
+                a = t + flip * (OFF - 1 - 2 * t)
+                tiles.append((n, a, halves[n], b, [(m + t, m) for m in range(rows - t)]))
+    multiply(tiles, weights, shifted, sums)
+
+
+def halo_kernel(halves, place, *refs):
+    *blocks, weights, earlier, total, pad, shifted = refs
+    rows = blocks[0].shape[0]
+    flip = place[2]
+
+    def body(sums):
+        halo_terms(place, blocks, [place[h] for h in halves], weights, pad, shifted, sums)
+        for m in range(rows):
+            i = m + flip * (rows - 1 - 2 * m)
+            total[i] = earlier[i] + collect(sums, m)
+
+    with_sums(rows, body)
+
+
+def last_kernel(halves, place, *refs):
+    *blocks, weights, earlier, source, image, pad, shifted = refs
+    rows = blocks[0].shape[0]
+    flip = place[2]
+
+    def body(sums):
+        halo_terms(place, blocks, [place[h] for h in halves], weights, pad, shifted, sums)
+        for m in range(rows):
+            i = m + flip * (rows - 1 - 2 * m)
+            coupled = (earlier[i] + collect(sums, m)).T
+            image[i] = (source[i].astype(jnp.float32) - coupled).astype(jnp.bfloat16)
+
+    with_sums(rows, body)
+
+
+def run(body, name, place, operands, blocks, rows, shape, dtype, tiles):
+    vmem = pl.BlockSpec(memory_space=pltpu.VMEM)
+    return pl.pallas_call(
+        body,
+        out_shape=jax.ShapeDtypeStruct(shape, dtype),
+        in_specs=[pl.BlockSpec(memory_space=pltpu.SMEM)] + [vmem] * len(operands),
+        out_specs=vmem,
+        scratch_shapes=[
+            pltpu.VMEM((rows, MXU // LANES, LANES + 2 * EDGE, LANES), jnp.float32),
+            pltpu.VMEM((blocks, OFF, rows, LANES, MXU), jnp.bfloat16),
+        ],
+        compiler_params=pltpu.CompilerParams(vmem_limit_bytes=16 << 20),
+        cost_estimate=pl.CostEstimate(
+            flops=2 * tiles * LANES * MXU * MXU, bytes_accessed=0, transcendentals=0
+        ),
+        name=name,
+    )(place, *operands)
+
+
+def paired(source, kernel):
+    devices = lax.axis_size("space")
+    here, half = lax.axis_index("space"), lax.axis_index("chan")
+    own = jnp.transpose(source, (1, 0, 2))
+    rows = own.shape[0]
+    swap = [(0, 1), (1, 0)]
+    near = [(i, i ^ 1) for i in range(devices) if i ^ 1 < devices]
+    far = [(i, ((i + 1) ^ 1) - 1) for i in range(devices)]
+    far = [(i, j) for i, j in far if 0 <= j < devices]
+    even = (1 - here % 2).astype(jnp.int32)
+    place_near = jnp.stack([half, 1 - half, even]).astype(jnp.int32)
+    place_far = jnp.stack([half, 1 - half, 1 - even]).astype(jnp.int32)
+
+    other = lax.ppermute(own, "chan", swap)
+    near_own = lax.ppermute(own, "space", near)
+    far_own = lax.ppermute(own, "space", far)
+    near_other = lax.ppermute(near_own, "chan", swap)
+    far_other = lax.ppermute(far_own, "chan", swap)
+
+    steps = 2 * OFF * sum(range(rows + 1))
+    sums = (rows, LANES, MXU)
+    total = run(
+        own_kernel, "own", place_near, [own, other, kernel], 2, rows, sums, jnp.float32,
+        2 * OFF * rows * rows,
+    )
+    total = run(
+        functools.partial(halo_kernel, (0, 1)), "near", place_near,
+        [near_own, near_other, kernel, total], 2, rows, sums, jnp.float32, steps,
+    )
+    total = run(
+        functools.partial(halo_kernel, (0,)), "far_own", place_far,
+        [far_own, kernel, total], 1, rows, sums, jnp.float32, steps // 2,
+    )
+    image = run(
+        functools.partial(last_kernel, (1,)), "far_other", place_far,
+        [far_other, kernel, total, own], 1, rows, own.shape, jnp.bfloat16, steps // 2,
+    )
+    return jnp.transpose(image, (1, 0, 2))
+
+
+def shards(source, kernel):
+    channels, rows, columns = source.shape
+    fits = channels == MXU and columns == LANES and rows == REACH
+    if lax.axis_size("chan") == 2 and fits and kernel.shape[2] == MXU:
+        return paired(source, kernel)
+    return general(source, kernel)
 
 
 def solution(mesh):

time: 40.6 us -> 30.2 us (0.74)
  the two profiles are of different devices: /device:TPU:0 before, /device:TPU:3 now
where the time goes in v1:
time: 30.2 us; the launch traced here: 30 us
  starting transfers between devices  10.9 us (36%)
  Pallas kernels  9.65 us (32%)
  local copies, waits for them, and re-layouts  6.87 us (23%)
  waiting for transfers between devices  2.27 us (8%)
    pallas_call x4, Pallas kernels, run(): pl.pallas_call(body, out_shape=jax.ShapeDtypeStruct(shape, dtype), in_spe...  9.65 us
    unnamed x8, local copies, waits for them, and re-layouts  6.87 us
    ppermute x1, starting transfers between devices, paired(): near_other = lax.ppermute(near_own, 'chan', swap)  5.07 us
    ppermute x1, starting transfers between devices, paired(): far_own = lax.ppermute(own, 'space', far)  4.32 us
    ppermute x1, waiting for transfers between devices, paired(): near_own = lax.ppermute(own, 'space', near)  2.17 us
    ppermute x1, starting transfers between devices, paired(): far_other = lax.ppermute(far_own, 'chan', swap)  0.86 us
    ppermute x1, starting transfers between devices, paired(): other = lax.ppermute(own, 'chan', swap)  0.68 us
  transfers between devices with their start and end apart: 5, of which 2 were waited for; matrix products, arithmetic and copies ran while one was open for 1% of the time, Pallas kernels for 24%

profile of v1, /device:TPU:3, one launch (start us, length us, event | category | flops | bytes accessed | tf_op | source)
XLA Modules:
  0.0 30.0 jit_solution(1720852036739781895)
XLA Ops:
  0.0 0.7 %collective-permute-start.4 = (bf16[3,256,128]{2,1,0:T(8,128)(2,1)}, bf16[3,256,128]{2,1,0:T(8,128)(2,1)S(1)}, u32[]{:S(2)}, u32[]{:S(2)}) collective-permute-start(bf16[3,256,128]{2,1,0:T(8,128)(2,1)} %bitcast.6), channel_id=1, source_target_pairs={{0,1},{1,0},{2,3},{3,2},{4,5},{5,4},{6,7},{7,6},{8,9},{9,8},{10,11... | collective-permute-start | bytes 589832 | tf_op jit(solution)/shard_map/ppermute | solution.py:209
  0.7 0.0 collective-permute-start.2
  0.7 4.3 %collective-permute-start = (bf16[3,256,128]{2,1,0:T(8,128)(2,1)}, bf16[3,256,128]{2,1,0:T(8,128)(2,1)S(1)}, u32[]{:S(2)}, u32[]{:S(2)}) collective-permute-start(bf16[3,256,128]{2,1,0:T(8,128)(2,1)} %bitcast.8), channel_id=1, source_target_pairs={{2,4},{4,2},{6,8},{8,6},{10,12},{12,10},{14,16},{16,14},{18,20},{2... | collective-permute-start | bytes 589832 | tf_op jit(solution)/shard_map/ppermute | solution.py:211
  5.0 0.1 pad_add_fusion.2.place
  5.1 0.1 pad_add_fusion.place
  5.2 2.2 %collective-permute-done.2.refs_0_ = bf16[3,256,128]{2,1,0:T(8,128)(2,1)S(1)} collective-permute-done((bf16[3,256,128]{2,1,0:T(8,128)(2,1)}, bf16[3,256,128]{2,1,0:T(8,128)(2,1)S(1)}, u32[]{:S(2)}, u32[]{:S(2)}) %collective-permute-start.2) | collective-permute-done | bytes 196640 | tf_op jit(solution)/shard_map/ppermute | solution.py:210
  7.3 5.1 %collective-permute-start.3 = (bf16[3,256,128]{2,1,0:T(8,128)(2,1)S(1)}, bf16[3,256,128]{2,1,0:T(8,128)(2,1)S(1)}, u32[]{:S(2)}, u32[]{:S(2)}) collective-permute-start(bf16[3,256,128]{2,1,0:T(8,128)(2,1)S(1)} %collective-permute-done.2.refs_0_), channel_id=1, source_target_pairs={{0,1},{1,0},{2,3},{3,2},{4,5},{5,4},{6,7},{7,6},{8,9},{9,8},{10,11... | collective-permute-start | bytes 589832 | tf_op jit(solution)/shard_map/ppermute | solution.py:212
  12.4 0.1 collective-permute-done.refs_0_
  12.5 0.9 %collective-permute-start.1 = (bf16[3,256,128]{2,1,0:T(8,128)(2,1)S(1)}, bf16[3,256,128]{2,1,0:T(8,128)(2,1)S(1)}, u32[]{:S(2)}, u32[]{:S(2)}) collective-permute-start(bf16[3,256,128]{2,1,0:T(8,128)(2,1)S(1)} %collective-permute-done.refs_0_), channel_id=1, source_target_pairs={{0,1},{1,0},{2,3},{3,2},{4,5},{5,4},{6,7},{7,6},{8,9},{9,8},{10,11... | collective-permute-start | bytes 589832 | tf_op jit(solution)/shard_map/ppermute | solution.py:213
  13.4 0.0 collective-permute-done.4.refs_1_
  13.4 0.0 copy-start
  13.4 4.6 %copy-done = bf16[7,7,256,512]{3,2,1,0:T(8,128)(2,1)S(1)} copy-done((bf16[7,7,256,512]{3,2,1,0:T(8,128)(2,1)S(1)}, bf16[7,7,256,512]{3,2,1,0:T(8,128)(2,1)}, u32[]{:S(2)}) %copy-start) | copy-done | bytes 12845080
  18.0 0.0 copy-start.2
  18.0 0.9 %copy-done.2 = bf16[256,3,128]{2,0,1:T(8,128)(2,1)S(1)} copy-done((bf16[256,3,128]{2,0,1:T(8,128)(2,1)S(1)}, bf16[256,3,128]{2,0,1:T(8,128)(2,1)}, u32[]{:S(2)}) %copy-start.2) | copy-done | bytes 196632
  19.0 0.0 copy-start.1
  19.0 3.3 %own.1.refs_3_ = f32[3,128,256]{2,1,0:T(8,128)S(1)} custom-call(s32[3]{0:T(128)S(1)} %pad_add_fusion.2.place, bf16[3,256,128]{2,1,0:T(8,128)(2,1)S(1)} %bitcast.9, bf16[3,256,128]{2,1,0:T(8,128)(2,1)S(1)} %collective-permute-done.4.refs_1_, bf16[7,7,256,512]{3,2,1,0:T(8,128)(2,1)S(1)} %copy-done), custom_call_target="tpu_custom_call" | custom-call | flops 2113929216 | tf_op jit(solution)/shard_map/own/pallas_call | solution.py:179
  22.3 0.0 copy-start.3
  22.3 0.0 collective-permute-done.3.refs_1_
  22.3 1.3 %copy-done.1 = bf16[7,7,256,512]{3,2,1,0:T(8,128)(2,1)S(1)} copy-done((bf16[7,7,256,512]{3,2,1,0:T(8,128)(2,1)S(1)}, bf16[7,7,256,512]{3,2,1,0:T(8,128)(2,1)}, u32[]{:S(2)}) %copy-start.1) | copy-done | bytes 12845080
  23.6 2.4 %near.1.refs_2_ = f32[3,128,256]{2,1,0:T(8,128)S(1)} custom-call(s32[3]{0:T(128)S(1)} %pad_add_fusion.2.place, bf16[3,256,128]{2,1,0:T(8,128)(2,1)S(1)} %collective-permute-done.2.refs_0_, bf16[3,256,128]{2,1,0:T(8,128)(2,1)S(1)} %collective-permute-done.3.refs_1_, bf16[7,7,256,512]{3,2,1,0:T(8,128)(2,1)S(1)} %copy-done.1, f32[3,128,256]{2,1,0:T(8,128)S(1)} %own.1.refs_3_), custom_call_target="tpu_custom_call" | custom-call | flops 1409286144 | tf_op jit(solution)/shard_map/near/pallas_call | solution.py:179
  26.0 1.5 %far_own.1.refs_2_ = f32[3,128,256]{2,1,0:T(8,128)S(1)} custom-call(s32[3]{0:T(128)S(1)} %pad_add_fusion.place, bf16[3,256,128]{2,1,0:T(8,128)(2,1)S(1)} %collective-permute-done.refs_0_, bf16[7,7,256,512]{3,2,1,0:T(8,128)(2,1)S(1)} %copy-done.1, f32[3,128,256]{2,1,0:T(8,128)S(1)} %near.1.refs_2_), custom_call_target="tpu_custom_call" | custom-call | flops 704643072 | tf_op jit(solution)/shard_map/far_own/pallas_call | solution.py:179
  27.6 0.0 collective-permute-done.1.refs_0_
  27.6 0.0 copy-done.3
  27.6 2.4 %far_other.1 = bf16[3,256,128]{2,1,0:T(8,128)(2,1)} custom-call(s32[3]{0:T(128)S(1)} %pad_add_fusion.place, bf16[3,256,128]{2,1,0:T(8,128)(2,1)S(1)} %collective-permute-done.1.refs_0_, bf16[7,7,256,512]{3,2,1,0:T(8,128)(2,1)S(1)} %copy-done.1, f32[3,128,256]{2,1,0:T(8,128)S(1)} %far_own.1.refs_2_, bf16[3,256,128]{2,1,0:T(8,128)(2,1)S(1)} %bitcast.10), custom_call_target="tpu_custom_call" | custom-call | flops 704643072 | tf_op jit(solution)/shard_map/far_other/pallas_call | solution.py:179
Async XLA Ops:
  0.0 13.4 %collective-permute-start.4 = (bf16[3,256,128]{2,1,0:T(8,128)(2,1)}, bf16[3,256,128]{2,1,0:T(8,128)(2,1)S(1)}, u32[]{:S(2)}, u32[]{:S(2)}) collective-permute-start(bf16[3,256,128]{2,1,0:T(8,128)(2,1)} %bitcast.6), channel_id=1, source_target_pairs={{0,1},{1,0},{2,3},{3,2},{4,5},{5,4},{6,7},{7,6},{8,9},{9,8},{10,11... | collective-permute-start | bytes 589832 | tf_op jit(solution)/shard_map/ppermute | solution.py:209
  0.7 6.7 %collective-permute-start.2 = (bf16[3,256,128]{2,1,0:T(8,128)(2,1)}, bf16[3,256,128]{2,1,0:T(8,128)(2,1)S(1)}, u32[]{:S(2)}, u32[]{:S(2)}) collective-permute-start(bf16[3,256,128]{2,1,0:T(8,128)(2,1)} %bitcast.7), channel_id=1, source_target_pairs={{0,2},{2,0},{4,6},{6,4},{8,10},{10,8},{12,14},{14,12},{16,18},{18,... | collective-permute-start | bytes 589832 | tf_op jit(solution)/shard_map/ppermute | solution.py:210
  0.7 11.8 %collective-permute-start = (bf16[3,256,128]{2,1,0:T(8,128)(2,1)}, bf16[3,256,128]{2,1,0:T(8,128)(2,1)S(1)}, u32[]{:S(2)}, u32[]{:S(2)}) collective-permute-start(bf16[3,256,128]{2,1,0:T(8,128)(2,1)} %bitcast.8), channel_id=1, source_target_pairs={{2,4},{4,2},{6,8},{8,6},{10,12},{12,10},{14,16},{16,14},{18,20},{2... | collective-permute-start | bytes 589832 | tf_op jit(solution)/shard_map/ppermute | solution.py:211
  7.3 15.0 %collective-permute-start.3 = (bf16[3,256,128]{2,1,0:T(8,128)(2,1)S(1)}, bf16[3,256,128]{2,1,0:T(8,128)(2,1)S(1)}, u32[]{:S(2)}, u32[]{:S(2)}) collective-permute-start(bf16[3,256,128]{2,1,0:T(8,128)(2,1)S(1)} %collective-permute-done.2.refs_0_), channel_id=1, source_target_pairs={{0,1},{1,0},{2,3},{3,2},{4,5},{5,4},{6,7},{7,6},{8,9},{9,8},{10,11... | collective-permute-start | bytes 589832 | tf_op jit(solution)/shard_map/ppermute | solution.py:212
  12.5 15.1 %collective-permute-start.1 = (bf16[3,256,128]{2,1,0:T(8,128)(2,1)S(1)}, bf16[3,256,128]{2,1,0:T(8,128)(2,1)S(1)}, u32[]{:S(2)}, u32[]{:S(2)}) collective-permute-start(bf16[3,256,128]{2,1,0:T(8,128)(2,1)S(1)} %collective-permute-done.refs_0_), channel_id=1, source_target_pairs={{0,1},{1,0},{2,3},{3,2},{4,5},{5,4},{6,7},{7,6},{8,9},{9,8},{10,11... | collective-permute-start | bytes 589832 | tf_op jit(solution)/shard_map/ppermute | solution.py:213
  13.4 4.7 %copy-start = (bf16[7,7,256,512]{3,2,1,0:T(8,128)(2,1)S(1)}, bf16[7,7,256,512]{3,2,1,0:T(8,128)(2,1)}, u32[]{:S(2)}) copy-start(bf16[7,7,256,512]{3,2,1,0:T(8,128)(2,1)} %refs_1_.3) | copy-start | bytes 38535172
  18.0 0.9 %copy-start.2 = (bf16[256,3,128]{2,0,1:T(8,128)(2,1)S(1)}, bf16[256,3,128]{2,0,1:T(8,128)(2,1)}, u32[]{:S(2)}) copy-start(bf16[256,3,128]{2,0,1:T(8,128)(2,1)} %param.2) | copy-start | bytes 589828
  19.0 4.7 %copy-start.1 = (bf16[7,7,256,512]{3,2,1,0:T(8,128)(2,1)S(1)}, bf16[7,7,256,512]{3,2,1,0:T(8,128)(2,1)}, u32[]{:S(2)}) copy-start(bf16[7,7,256,512]{3,2,1,0:T(8,128)(2,1)} %refs_1_.3) | copy-start | bytes 38535172
  22.3 5.3 %copy-start.3 = (bf16[256,3,128]{2,0,1:T(8,128)(2,1)S(1)}, bf16[256,3,128]{2,0,1:T(8,128)(2,1)}, u32[]{:S(2)}) copy-start(bf16[256,3,128]{2,0,1:T(8,128)(2,1)} %param.2) | copy-start | bytes 589828

commit v2 on v1

--- a/solution.py
+++ b/solution.py
@@ -13,6 +13,8 @@
 LANES = 128
 EDGE = 8
 UNITS = 2
+FIRST = 2 * 10**9
+SECOND = 2 * 10**9
 
 
 def padded_2(array, sides, width):
@@ -108,7 +110,14 @@
     pl.run_scoped(lambda *sums: body(sums), *refs)
 
 
-def own_kernel(place, *refs):
+def place_of(side):
+    half = lax.axis_index("chan")
+    odd = lax.axis_index("space") % 2
+    return half, 1 - half, odd if side == "far" else 1 - odd
+
+
+def own_kernel(*refs):
+    place = place_of("own")
     *blocks, weights, total, pad, shifted = refs
     rows = blocks[0].shape[0]
 
@@ -145,7 +154,8 @@
     multiply(tiles, weights, shifted, sums)
 
 
-def halo_kernel(halves, place, *refs):
+def halo_kernel(side, halves, *refs):
+    place = place_of(side)
     *blocks, weights, earlier, total, pad, shifted = refs
     rows = blocks[0].shape[0]
     flip = place[2]
@@ -159,7 +169,8 @@
     with_sums(rows, body)
 
 
-def last_kernel(halves, place, *refs):
+def last_kernel(side, halves, *refs):
+    place = place_of(side)
     *blocks, weights, earlier, source, image, pad, shifted = refs
     rows = blocks[0].shape[0]
     flip = place[2]
@@ -174,12 +185,12 @@
     with_sums(rows, body)
 
 
-def run(body, name, place, operands, blocks, rows, shape, dtype, tiles):
+def run(body, operands, blocks, rows, shape, dtype, tiles):
     vmem = pl.BlockSpec(memory_space=pltpu.VMEM)
     return pl.pallas_call(
         body,
         out_shape=jax.ShapeDtypeStruct(shape, dtype),
-        in_specs=[pl.BlockSpec(memory_space=pltpu.SMEM)] + [vmem] * len(operands),
+        in_specs=[vmem] * len(operands),
         out_specs=vmem,
         scratch_shapes=[
             pltpu.VMEM((rows, MXU // LANES, LANES + 2 * EDGE, LANES), jnp.float32),
@@ -189,45 +200,61 @@
         cost_estimate=pl.CostEstimate(
             flops=2 * tiles * LANES * MXU * MXU, bytes_accessed=0, transcendentals=0
         ),
-        name=name,
-    )(place, *operands)
+    )(*operands)
+
+
+def opening(cost):
+    def body(out):
+        del out
+
+    return pl.pallas_call(
+        body,
+        out_shape=jax.ShapeDtypeStruct((EDGE, LANES), jnp.float32),
+        out_specs=pl.BlockSpec(memory_space=pl.ANY),
+        compiler_params=pltpu.CompilerParams(vmem_limit_bytes=1 << 20, has_side_effects=True),
+        cost_estimate=pl.CostEstimate(flops=cost, bytes_accessed=0, transcendentals=0),
+    )()
 
 
 def paired(source, kernel):
     devices = lax.axis_size("space")
-    here, half = lax.axis_index("space"), lax.axis_index("chan")
+    first = opening(FIRST)
+    source, first = lax.optimization_barrier((source, first))
     own = jnp.transpose(source, (1, 0, 2))
     rows = own.shape[0]
     swap = [(0, 1), (1, 0)]
     near = [(i, i ^ 1) for i in range(devices) if i ^ 1 < devices]
     far = [(i, ((i + 1) ^ 1) - 1) for i in range(devices)]
     far = [(i, j) for i, j in far if 0 <= j < devices]
-    even = (1 - here % 2).astype(jnp.int32)
-    place_near = jnp.stack([half, 1 - half, even]).astype(jnp.int32)
-    place_far = jnp.stack([half, 1 - half, 1 - even]).astype(jnp.int32)
 
     other = lax.ppermute(own, "chan", swap)
     near_own = lax.ppermute(own, "space", near)
     far_own = lax.ppermute(own, "space", far)
-    near_other = lax.ppermute(near_own, "chan", swap)
-    far_other = lax.ppermute(far_own, "chan", swap)
+    second = opening(SECOND)
+    own, second = lax.optimization_barrier((own, second))
 
     steps = 2 * OFF * sum(range(rows + 1))
     sums = (rows, LANES, MXU)
     total = run(
-        own_kernel, "own", place_near, [own, other, kernel], 2, rows, sums, jnp.float32,
+        own_kernel, [own, other, kernel], 2, rows, sums, jnp.float32,
         2 * OFF * rows * rows,
     )
-    total = run(
-        functools.partial(halo_kernel, (0, 1)), "near", place_near,
-        [near_own, near_other, kernel, total], 2, rows, sums, jnp.float32, steps,
-    )
-    total = run(
-        functools.partial(halo_kernel, (0,)), "far_own", place_far,
+    near_other = lax.ppermute(near_own, "chan", swap)
+    total = run(
+        functools.partial(halo_kernel, "near", (0,)),
+        [near_own, kernel, total], 1, rows, sums, jnp.float32, steps // 2,
+    )
+    total = run(
+        functools.partial(halo_kernel, "near", (1,)),
+        [near_other, kernel, total], 1, rows, sums, jnp.float32, steps // 2,
+    )
+    far_other = lax.ppermute(far_own, "chan", swap)
+    total = run(
+        functools.partial(halo_kernel, "far", (0,)),
         [far_own, kernel, total], 1, rows, sums, jnp.float32, steps // 2,
     )
     image = run(
-        functools.partial(last_kernel, (1,)), "far_other", place_far,
+        functools.partial(last_kernel, "far", (1,)),
         [far_other, kernel, total, own], 1, rows, own.shape, jnp.bfloat16, steps // 2,
     )
     return jnp.transpose(image, (1, 0, 2))

time: 30.2 us -> 20.7 us (0.69)
  the two profiles are of different devices: /device:TPU:3 before, /device:TPU:19 now
where the time goes in v2:
time: 20.7 us; the launch traced here: 20.6 us
  starting transfers between devices  9.01 us (44%)
  Pallas kernels  7.77 us (38%)
  waiting for transfers between devices  3.75 us (18%)
    pallas_call x5, Pallas kernels, run(): pl.pallas_call(body, out_shape=jax.ShapeDtypeStruct(shape, dtype), in_spe...  7.77 us
    ppermute x1, starting transfers between devices, paired(): far_own = lax.ppermute(own, 'space', far)  4.33 us
    ppermute x1, waiting for transfers between devices, paired(): far_own = lax.ppermute(own, 'space', far)  3.64 us
    ppermute x1, starting transfers between devices, paired(): near_other = lax.ppermute(near_own, 'chan', swap)  1.53 us
    ppermute x1, starting transfers between devices, paired(): far_other = lax.ppermute(far_own, 'chan', swap)  1.53 us
    ppermute x1, starting transfers between devices, paired(): other = lax.ppermute(own, 'chan', swap)  1.3 us
  transfers between devices with their start and end apart: 5, of which 2 were waited for; matrix products, arithmetic and copies ran while one was open for 0% of the time, Pallas kernels for 29%

profile of v2, /device:TPU:19, one launch (start us, length us, event | category | flops | bytes accessed | tf_op | source)
XLA Modules:
  0.0 20.6 jit_solution(1209873901212365957)
XLA Ops:
  0.0 0.0 copy-start.1
  0.0 0.0 copy-start
  0.0 0.3 %collective-permute-start.2 = (bf16[3,256,128]{2,1,0:T(8,128)(2,1)}, bf16[3,256,128]{2,1,0:T(8,128)(2,1)S(1)}, u32[]{:S(2)}, u32[]{:S(2)}) collective-permute-start(bf16[3,256,128]{2,1,0:T(8,128)(2,1)} %bitcast.2), channel_id=1, source_target_pairs={{0,2},{2,0},{4,6},{6,4},{8,10},{10,8},{12,14},{14,12},{16,18},{18,... | collective-permute-start | bytes 589832 | tf_op jit(solution)/shard_map/ppermute | solution.py:231
  0.3 4.3 %collective-permute-start = (bf16[3,256,128]{2,1,0:T(8,128)(2,1)}, bf16[3,256,128]{2,1,0:T(8,128)(2,1)S(1)}, u32[]{:S(2)}, u32[]{:S(2)}) collective-permute-start(bf16[3,256,128]{2,1,0:T(8,128)(2,1)} %bitcast.3), channel_id=1, source_target_pairs={{2,4},{4,2},{6,8},{8,6},{10,12},{12,10},{14,16},{16,14},{18,20},{2... | collective-permute-start | bytes 589832 | tf_op jit(solution)/shard_map/ppermute | solution.py:232
  4.7 1.3 %collective-permute-start.4 = (bf16[3,256,128]{2,1,0:T(8,128)(2,1)}, bf16[3,256,128]{2,1,0:T(8,128)(2,1)S(1)}, u32[]{:S(2)}, u32[]{:S(2)}) collective-permute-start(bf16[3,256,128]{2,1,0:T(8,128)(2,1)} %bitcast.4), channel_id=1, source_target_pairs={{0,1},{1,0},{2,3},{3,2},{4,5},{5,4},{6,7},{7,6},{8,9},{9,8},{10,11... | collective-permute-start | bytes 589832 | tf_op jit(solution)/shard_map/ppermute | solution.py:230
  6.0 0.1 collective-permute-done.2.refs_0_
  6.1 1.5 %collective-permute-start.3 = (bf16[3,256,128]{2,1,0:T(8,128)(2,1)S(1)}, bf16[3,256,128]{2,1,0:T(8,128)(2,1)S(1)}, u32[]{:S(2)}, u32[]{:S(2)}) collective-permute-start(bf16[3,256,128]{2,1,0:T(8,128)(2,1)S(1)} %collective-permute-done.2.refs_0_), channel_id=1, source_target_pairs={{0,1},{1,0},{2,3},{3,2},{4,5},{5,4},{6,7},{7,6},{8,9},{9,8},{10,11... | collective-permute-start | bytes 589832 | tf_op jit(solution)/shard_map/ppermute | solution.py:242
  7.6 3.6 %collective-permute-done.refs_0_ = bf16[3,256,128]{2,1,0:T(8,128)(2,1)S(1)} collective-permute-done((bf16[3,256,128]{2,1,0:T(8,128)(2,1)}, bf16[3,256,128]{2,1,0:T(8,128)(2,1)S(1)}, u32[]{:S(2)}, u32[]{:S(2)}) %collective-permute-start) | collective-permute-done | bytes 196640 | tf_op jit(solution)/shard_map/ppermute | solution.py:232
  11.2 1.5 %collective-permute-start.1 = (bf16[3,256,128]{2,1,0:T(8,128)(2,1)S(1)}, bf16[3,256,128]{2,1,0:T(8,128)(2,1)S(1)}, u32[]{:S(2)}, u32[]{:S(2)}) collective-permute-start(bf16[3,256,128]{2,1,0:T(8,128)(2,1)S(1)} %collective-permute-done.refs_0_), channel_id=1, source_target_pairs={{0,1},{1,0},{2,3},{3,2},{4,5},{5,4},{6,7},{7,6},{8,9},{9,8},{10,11... | collective-permute-start | bytes 589832 | tf_op jit(solution)/shard_map/ppermute | solution.py:251
  12.8 0.0 collective-permute-done.4.refs_1_
  12.8 0.0 copy-done.1
  12.8 0.0 copy-done
  12.8 2.8 %shard_map.30.refs_2_ = f32[3,128,256]{2,1,0:T(8,128)S(1)} custom-call(bf16[3,256,128]{2,1,0:T(8,128)(2,1)S(1)} %bitcast.5, bf16[3,256,128]{2,1,0:T(8,128)(2,1)S(1)} %collective-permute-done.4.refs_1_, bf16[7,7,256,512]{3,2,1,0:T(8,128)(2,1)S(1)} %copy-done), custom_call_target="tpu_custom_call" | custom-call | flops 2113929216 | tf_op jit(solution)/shard_map/pallas_call | solution.py:190
  15.6 1.1 %shard_map.31.refs_2_ = f32[3,128,256]{2,1,0:T(8,128)S(1)} custom-call(bf16[3,256,128]{2,1,0:T(8,128)(2,1)S(1)} %collective-permute-done.2.refs_0_, bf16[7,7,256,512]{3,2,1,0:T(8,128)(2,1)S(1)} %copy-done, f32[3,128,256]{2,1,0:T(8,128)S(1)} %shard_map.30.refs_2_), custom_call_target="tpu_custom_call" | custom-call | flops 704643072 | tf_op jit(solution)/shard_map/pallas_call | solution.py:190
  16.7 0.0 collective-permute-done.3.refs_0_
  16.7 1.0 %shard_map.32.refs_2_ = f32[3,128,256]{2,1,0:T(8,128)S(1)} custom-call(bf16[3,256,128]{2,1,0:T(8,128)(2,1)S(1)} %collective-permute-done.3.refs_0_, bf16[7,7,256,512]{3,2,1,0:T(8,128)(2,1)S(1)} %copy-done, f32[3,128,256]{2,1,0:T(8,128)S(1)} %shard_map.31.refs_2_), custom_call_target="tpu_custom_call" | custom-call | flops 704643072 | tf_op jit(solution)/shard_map/pallas_call | solution.py:190
  17.7 1.1 %shard_map.33.refs_2_ = f32[3,128,256]{2,1,0:T(8,128)S(1)} custom-call(bf16[3,256,128]{2,1,0:T(8,128)(2,1)S(1)} %collective-permute-done.refs_0_, bf16[7,7,256,512]{3,2,1,0:T(8,128)(2,1)S(1)} %copy-done, f32[3,128,256]{2,1,0:T(8,128)S(1)} %shard_map.32.refs_2_), custom_call_target="tpu_custom_call" | custom-call | flops 704643072 | tf_op jit(solution)/shard_map/pallas_call | solution.py:190
  18.8 0.0 collective-permute-done.1.refs_0_
  18.8 1.8 %shard_map.34 = bf16[3,256,128]{2,1,0:T(8,128)(2,1)} custom-call(bf16[3,256,128]{2,1,0:T(8,128)(2,1)S(1)} %collective-permute-done.1.refs_0_, bf16[7,7,256,512]{3,2,1,0:T(8,128)(2,1)S(1)} %copy-done, f32[3,128,256]{2,1,0:T(8,128)S(1)} %shard_map.33.refs_2_, bf16[3,256,128]{2,1,0:T(8,128)(2,1)S(1)} %bitcast.6), custom_call_target="tpu_custom_call" | custom-call | flops 704643072 | tf_op jit(solution)/shard_map/pallas_call | solution.py:190
  (2 shorter events, 0.0 us)
Async XLA Ops:
  0.0 12.8 %copy-start.1 = (bf16[256,3,128]{2,0,1:T(8,128)(2,1)S(1)}, bf16[256,3,128]{2,0,1:T(8,128)(2,1)}, u32[]{:S(2)}) copy-start(bf16[256,3,128]{2,0,1:T(8,128)(2,1)} %param.2) | copy-start | bytes 589828
  0.0 12.8 %copy-start = (bf16[7,7,256,512]{3,2,1,0:T(8,128)(2,1)S(1)}, bf16[7,7,256,512]{3,2,1,0:T(8,128)(2,1)}, u32[]{:S(2)}) copy-start(bf16[7,7,256,512]{3,2,1,0:T(8,128)(2,1)} %refs_1_.7) | copy-start | bytes 38535172
  0.0 6.1 %collective-permute-start.2 = (bf16[3,256,128]{2,1,0:T(8,128)(2,1)}, bf16[3,256,128]{2,1,0:T(8,128)(2,1)S(1)}, u32[]{:S(2)}, u32[]{:S(2)}) collective-permute-start(bf16[3,256,128]{2,1,0:T(8,128)(2,1)} %bitcast.2), channel_id=1, source_target_pairs={{0,2},{2,0},{4,6},{6,4},{8,10},{10,8},{12,14},{14,12},{16,18},{18,... | collective-permute-start | bytes 589832 | tf_op jit(solution)/shard_map/ppermute | solution.py:231
  0.3 10.9 %collective-permute-start = (bf16[3,256,128]{2,1,0:T(8,128)(2,1)}, bf16[3,256,128]{2,1,0:T(8,128)(2,1)S(1)}, u32[]{:S(2)}, u32[]{:S(2)}) collective-permute-start(bf16[3,256,128]{2,1,0:T(8,128)(2,1)} %bitcast.3), channel_id=1, source_target_pairs={{2,4},{4,2},{6,8},{8,6},{10,12},{12,10},{14,16},{16,14},{18,20},{2... | collective-permute-start | bytes 589832 | tf_op jit(solution)/shard_map/ppermute | solution.py:232
  4.7 8.1 %collective-permute-start.4 = (bf16[3,256,128]{2,1,0:T(8,128)(2,1)}, bf16[3,256,128]{2,1,0:T(8,128)(2,1)S(1)}, u32[]{:S(2)}, u32[]{:S(2)}) collective-permute-start(bf16[3,256,128]{2,1,0:T(8,128)(2,1)} %bitcast.4), channel_id=1, source_target_pairs={{0,1},{1,0},{2,3},{3,2},{4,5},{5,4},{6,7},{7,6},{8,9},{9,8},{10,11... | collective-permute-start | bytes 589832 | tf_op jit(solution)/shard_map/ppermute | solution.py:230
  6.1 10.6 %collective-permute-start.3 = (bf16[3,256,128]{2,1,0:T(8,128)(2,1)S(1)}, bf16[3,256,128]{2,1,0:T(8,128)(2,1)S(1)}, u32[]{:S(2)}, u32[]{:S(2)}) collective-permute-start(bf16[3,256,128]{2,1,0:T(8,128)(2,1)S(1)} %collective-permute-done.2.refs_0_), channel_id=1, source_target_pairs={{0,1},{1,0},{2,3},{3,2},{4,5},{5,4},{6,7},{7,6},{8,9},{9,8},{10,11... | collective-permute-start | bytes 589832 | tf_op jit(solution)/shard_map/ppermute | solution.py:242
  11.2 7.6 %collective-permute-start.1 = (bf16[3,256,128]{2,1,0:T(8,128)(2,1)S(1)}, bf16[3,256,128]{2,1,0:T(8,128)(2,1)S(1)}, u32[]{:S(2)}, u32[]{:S(2)}) collective-permute-start(bf16[3,256,128]{2,1,0:T(8,128)(2,1)S(1)} %collective-permute-done.refs_0_), channel_id=1, source_target_pairs={{0,1},{1,0},{2,3},{3,2},{4,5},{5,4},{6,7},{7,6},{8,9},{9,8},{10,11... | collective-permute-start | bytes 589832 | tf_op jit(solution)/shard_map/ppermute | solution.py:251
